TPU v7x, 128 devices: a whole 4x4x4 slice. The times are simulated.
128 devices in a mesh: row: 8 (over z, core), col: 16 (over y, x).
Axes of the slice: x: 4, y: 4, z: 4, core: 2. Of those that a mesh axis runs over, the one named last changes fastest.
Arguments:
- symmetric: float32 [16384, 16384], P('row', 'col'), may hold values from -8 to 8, as said below
- reflectors: float32 [4, 64, 16384], P(None, None, ('row', 'col')), may hold values from -0.125 to 0.125
- tri_factor: float32 [4, 64, 64], replicated, may hold values from -0.4 to 1.5, as said below
Outputs:
- updated: float32 [16384, 16384], P('row', 'col')
Inputs may be any that keep to these rules, and one draw needn't show every extreme that they name: symmetric is a symmetric matrix. Each tri_factor[p] is upper triangular.
All inputs are finite; a program needn't handle non-finite values.
Results may differ from a plain program's by a relative error of at most 0.00029.
Values sent between devices are 32-bit elements; how exact they have to be, the bound alone decides.
A program may use at most 64 MiB of HBM per device.

v0:
```python
import jax
import jax.numpy as jnp
from jax import lax
from jax.sharding import PartitionSpec as P


def broadcast(value, axis, source):
    kept = jnp.where(lax.axis_index(axis) == source, value, 0).astype(value.dtype)
    return lax.psum(kept, axis)


def shards(symmetric, reflectors, tri_factor):
    highest = lax.Precision.HIGHEST
    cols_here = symmetric.shape[1]
    row_count = lax.axis_size("row")
    col_count = lax.axis_size("col")
    col_index = lax.axis_index("col")
    owner = col_index * row_count // col_count
    offset = col_index % (col_count // row_count) * cols_here
    matrix = symmetric
    for panel in range(reflectors.shape[0]):
        piece = reflectors[panel]
        factor = tri_factor[panel]
        reflect_rows = lax.all_gather(piece, "col", axis=1, tiled=True)
        reflect_cols = broadcast(
            lax.dynamic_slice_in_dim(reflect_rows, offset, cols_here, 1), "row", owner
        )
        partial_value = lax.dot_general(
            reflect_cols,
            matrix,
            (((1,), (1,)), ((), ())),
            precision=highest,
            preferred_element_type=jnp.float32,
        )
        product_rows = lax.psum(partial_value, "col")
        image_rows = jnp.dot(
            factor.T, product_rows, precision=highest, preferred_element_type=jnp.float32
        )
        local_inner = lax.dot_general(
            reflect_rows,
            image_rows,
            (((1,), (1,)), ((), ())),
            precision=highest,
            preferred_element_type=jnp.float32,
        )
        inner = lax.psum(local_inner, "row")
        coupling = jnp.dot(factor.T, inner, precision=highest, preferred_element_type=jnp.float32)
        update_rows = image_rows - 0.5 * jnp.dot(
            coupling.T, reflect_rows, precision=highest, preferred_element_type=jnp.float32
        )
        update_cols = broadcast(
            lax.dynamic_slice_in_dim(update_rows, offset, cols_here, 1), "row", owner
        )
        left_block = jnp.concatenate([reflect_rows, update_rows], axis=0)
        right_block = jnp.concatenate([update_cols, reflect_cols], axis=0)
        matrix = matrix - lax.dot_general(
            left_block,
            right_block,
            (((0,), (0,)), ((), ())),
            precision=highest,
            preferred_element_type=jnp.float32,
        )
    return matrix


def solution(mesh):
    placed = (P("row", "col"), P(None, None, ("row", "col")), P())
    return jax.shard_map(
        shards, mesh=mesh, in_specs=placed, out_specs=P("row", "col"), check_vma=False
    )
```

profile of v0, /device:TPU:0, one launch (start us, length us, event | category | flops | bytes accessed | tf_op | source)
XLA Modules:
  0.0 878.7 jit_solution(7771888216284126579)
XLA Ops:
  7.4 25.2 %all-gather = f32[1,64,2048]{2,1,0:T(8,128)S(1)} all-gather(f32[1,64,128]{2,1,0:T(8,128)S(1)} %get-tuple-element.13), channel_id=2, replica_groups=mesh['row'=8,'col'=16] {'col'}, dimensions={2}, use_global_device_ids=true | all-gather | bytes 557056 | tf_op jit(solution)/shard_map/all_gather | solution.py:24
  33.4 60.0 %all-reduce.13.cloned.1.call-done = f32[64,1024]{1,0:T(8,128)} async-done(((f32[64,1024]{1,0:T(8,128)}), f32[64,1024]{1,0:T(8,128)}) %all-reduce.13.cloned.1.call-update) | async-done | bytes 262160 | tf_op jit(solution)/shard_map/psum | solution.py:9
  93.4 12.3 %fusion.65 = f32[64,2048]{1,0:T(8,128)} fusion(f32[64,1024]{1,0:T(8,128)} %all-reduce.13.cloned.1.call-done, f32[2048,1024]{1,0:T(8,128)} %param.3), kind=kOutput, calls=%fused_computation.85 | convolution fusion | flops 1610612736 | bytes 9175040 | tf_op jit(solution)/shard_map/dot_general | solution.py:28
  105.7 25.3 %all-gather.1 = f32[1,64,2048]{2,1,0:T(8,128)S(1)} all-gather(f32[1,64,128]{2,1,0:T(8,128)S(1)} %get-tuple-element.12), channel_id=3, replica_groups=mesh['row'=8,'col'=16] {'col'}, dimensions={2}, use_global_device_ids=true | all-gather | bytes 557056 | tf_op jit(solution)/shard_map/all_gather | solution.py:24
  131.7 58.1 %all-reduce.15.cloned.1.call-done = f32[64,2048]{1,0:T(8,128)} async-done(((f32[64,2048]{1,0:T(8,128)}), f32[64,2048]{1,0:T(8,128)}) %all-reduce.15.cloned.1.call-update) | async-done | bytes 524304 | tf_op jit(solution)/shard_map/psum | solution.py:35
  189.9 1.7 fusion.42
  192.1 24.4 %psum.114 = f32[64,64]{0,1:T(8,128)S(1)} all-reduce(f32[64,64]{0,1:T(8,128)S(1)} %convolution_bitcast_fusion.3), channel_id=1, replica_groups=mesh['row'=8,'col'=16] {'row'}, use_global_device_ids=true, to_apply=%region_2.3 | all-reduce | flops 4096 | bytes 32768 | tf_op jit(solution)/shard_map/psum | solution.py:46
  218.3 57.3 %all-reduce.29.cloned.1.call-done = (f32[64,1024]{1,0:T(8,128)}, f32[64,1024]{1,0:T(8,128)}) async-done(((f32[64,1024]{1,0:T(8,128)}, f32[64,1024]{1,0:T(8,128)}), (f32[64,1024]{1,0:T(8,128)}, f32[64,1024]{1,0:T(8,128)})) %all-reduce.29.cloned.1.call-update) | async-done | bytes 524304 | tf_op jit(solution)/shard_map/psum | solution.py:9
  275.6 12.9 %convolution_subtract_fusion.3 = f32[2048,1024]{1,0:T(8,128)S(1)} fusion(f32[2048,1024]{1,0:T(8,128)} %param.3, f32[64,2048]{1,0:T(8,128)S(1)} %fusion.3, f32[64,2048]{1,0:T(8,128)S(1)} %bitcast.91, f32[64,1024]{1,0:T(8,128)S(1)} %copy-done.6, f32[64,1024]{1,0:T(8,128)} %get-tuple-element.9), kind=kOutput, calls=%fused_computation.3 | convolution fusion | flops 3223715840 | bytes 18350080 | tf_op jit(solution)/shard_map/dot_general | solution.py:56
  288.5 3.4 copy-done.1
  291.9 8.9 %fusion.66 = f32[64,2048]{1,0:T(8,128)} fusion(f32[64,1024]{1,0:T(8,128)S(1)} %copy-done.4, f32[2048,1024]{1,0:T(8,128)S(1)} %convolution_subtract_fusion.3), kind=kOutput, calls=%fused_computation.86 | convolution fusion | flops 1610612736 | bytes 9175040 | tf_op jit(solution)/shard_map/dot_general | solution.py:28
  300.8 25.4 %all-gather.2 = f32[1,64,2048]{2,1,0:T(8,128)S(1)} all-gather(f32[1,64,128]{2,1,0:T(8,128)S(1)} %get-tuple-element.14), channel_id=4, replica_groups=mesh['row'=8,'col'=16] {'col'}, dimensions={2}, use_global_device_ids=true | all-gather | bytes 557056 | tf_op jit(solution)/shard_map/all_gather | solution.py:24
  327.0 58.3 %all-reduce.17.cloned.1.call-done = f32[64,2048]{1,0:T(8,128)} async-done(((f32[64,2048]{1,0:T(8,128)}), f32[64,2048]{1,0:T(8,128)}) %all-reduce.17.cloned.1.call-update) | async-done | bytes 524304 | tf_op jit(solution)/shard_map/psum | solution.py:35
  385.2 1.7 fusion.38
  387.5 24.4 %psum.118 = f32[64,64]{0,1:T(8,128)S(1)} all-reduce(f32[64,64]{0,1:T(8,128)S(1)} %convolution_bitcast_fusion.2), channel_id=1, replica_groups=mesh['row'=8,'col'=16] {'row'}, use_global_device_ids=true, to_apply=%region_6.7 | all-reduce | flops 4096 | bytes 32768 | tf_op jit(solution)/shard_map/psum | solution.py:46
  413.8 57.1 %all-reduce.27.cloned.1.call-done = (f32[64,1024]{1,0:T(8,128)}, f32[64,1024]{1,0:T(8,128)}) async-done(((f32[64,1024]{1,0:T(8,128)}, f32[64,1024]{1,0:T(8,128)}), (f32[64,1024]{1,0:T(8,128)}, f32[64,1024]{1,0:T(8,128)})) %all-reduce.27.cloned.1.call-update) | async-done | bytes 524304 | tf_op jit(solution)/shard_map/psum | solution.py:9
  471.0 12.9 %convolution_subtract_fusion.2 = f32[2048,1024]{1,0:T(8,128)S(1)} fusion(f32[2048,1024]{1,0:T(8,128)} %copy-done.1, f32[64,2048]{1,0:T(8,128)S(1)} %fusion.2, f32[64,2048]{1,0:T(8,128)S(1)} %bitcast.89, f32[64,1024]{1,0:T(8,128)S(1)} %copy-done.4, f32[64,1024]{1,0:T(8,128)} %get-tuple-element.7), kind=kOutput, calls=%fused_computation.2 | convolution fusion | flops 3223715840 | bytes 18350080 | tf_op jit(solution)/shard_map/dot_general | solution.py:56
  483.9 3.4 copy-done
  487.3 8.9 %fusion.67 = f32[64,2048]{1,0:T(8,128)} fusion(f32[64,1024]{1,0:T(8,128)S(1)} %copy-done.3, f32[2048,1024]{1,0:T(8,128)S(1)} %convolution_subtract_fusion.2), kind=kOutput, calls=%fused_computation.87 | convolution fusion | flops 1610612736 | bytes 9175040 | tf_op jit(solution)/shard_map/dot_general | solution.py:28
  496.2 25.4 %all-gather.3 = f32[1,64,2048]{2,1,0:T(8,128)S(1)} all-gather(f32[1,64,128]{2,1,0:T(8,128)S(1)} %get-tuple-element.11), channel_id=5, replica_groups=mesh['row'=8,'col'=16] {'col'}, dimensions={2}, use_global_device_ids=true | all-gather | bytes 557056 | tf_op jit(solution)/shard_map/all_gather | solution.py:24
  522.4 58.3 %all-reduce.19.cloned.1.call-done = f32[64,2048]{1,0:T(8,128)} async-done(((f32[64,2048]{1,0:T(8,128)}), f32[64,2048]{1,0:T(8,128)}) %all-reduce.19.cloned.1.call-update) | async-done | bytes 524304 | tf_op jit(solution)/shard_map/psum | solution.py:35
  580.6 1.7 fusion.34
  582.9 24.4 %psum.122 = f32[64,64]{0,1:T(8,128)S(1)} all-reduce(f32[64,64]{0,1:T(8,128)S(1)} %convolution_bitcast_fusion.1), channel_id=1, replica_groups=mesh['row'=8,'col'=16] {'row'}, use_global_device_ids=true, to_apply=%region_10.11 | all-reduce | flops 4096 | bytes 32768 | tf_op jit(solution)/shard_map/psum | solution.py:46
  609.0 57.3 %all-reduce.25.cloned.1.call-done = (f32[64,1024]{1,0:T(8,128)}, f32[64,1024]{1,0:T(8,128)}) async-done(((f32[64,1024]{1,0:T(8,128)}, f32[64,1024]{1,0:T(8,128)}), (f32[64,1024]{1,0:T(8,128)}, f32[64,1024]{1,0:T(8,128)})) %all-reduce.25.cloned.1.call-update) | async-done | bytes 524304 | tf_op jit(solution)/shard_map/psum | solution.py:9
  666.3 12.9 %convolution_subtract_fusion.1 = f32[2048,1024]{1,0:T(8,128)S(1)} fusion(f32[2048,1024]{1,0:T(8,128)} %copy-done, f32[64,2048]{1,0:T(8,128)S(1)} %fusion.1, f32[64,2048]{1,0:T(8,128)S(1)} %bitcast.88, f32[64,1024]{1,0:T(8,128)S(1)} %copy-done.3, f32[64,1024]{1,0:T(8,128)} %get-tuple-element.5), kind=kOutput, calls=%fused_computation.1 | convolution fusion | flops 3223715840 | bytes 18350080 | tf_op jit(solution)/shard_map/dot_general | solution.py:56
  679.2 3.4 copy-done.2
  682.6 8.9 %fusion.68 = f32[64,2048]{1,0:T(8,128)} fusion(f32[64,1024]{1,0:T(8,128)S(1)} %copy-done.5, f32[2048,1024]{1,0:T(8,128)S(1)} %convolution_subtract_fusion.1), kind=kOutput, calls=%fused_computation.88 | convolution fusion | flops 1610612736 | bytes 9175040 | tf_op jit(solution)/shard_map/dot_general | solution.py:28
  691.6 84.2 %all-reduce.21.cloned.1.call-done = f32[64,2048]{1,0:T(8,128)} async-done(((f32[64,2048]{1,0:T(8,128)}), f32[64,2048]{1,0:T(8,128)}) %all-reduce.21.cloned.1.call-update) | async-done | bytes 524304 | tf_op jit(solution)/shard_map/psum | solution.py:35
  775.8 1.7 fusion.30
  778.1 24.8 %psum.126 = f32[64,64]{0,1:T(8,128)S(1)} all-reduce(f32[64,64]{0,1:T(8,128)S(1)} %convolution_bitcast_fusion), channel_id=1, replica_groups=mesh['row'=8,'col'=16] {'row'}, use_global_device_ids=true, to_apply=%region_14.15 | all-reduce | flops 4096 | bytes 32768 | tf_op jit(solution)/shard_map/psum | solution.py:46
  804.3 56.4 %all-reduce.23.cloned.1.call-done = f32[64,1024]{1,0:T(8,128)} async-done(((f32[64,1024]{1,0:T(8,128)}), f32[64,1024]{1,0:T(8,128)}) %all-reduce.23.cloned.1.call-update) | async-done | bytes 262160 | tf_op jit(solution)/shard_map/psum | solution.py:9
  860.7 11.2 %convolution_subtract_fusion = f32[2048,1024]{1,0:T(8,128)} fusion(f32[2048,1024]{1,0:T(8,128)} %copy-done.2, f32[64,2048]{1,0:T(8,128)S(1)} %fusion, f32[64,2048]{1,0:T(8,128)S(1)} %bitcast.90, f32[64,1024]{1,0:T(8,128)S(1)} %copy-done.5, f32[64,1024]{1,0:T(8,128)} %all-reduce.23.cloned.1.call-done), kind=kOutput, calls=%fused_computation | convolution fusion | flops 3223715840 | bytes 18350080 | tf_op jit(solution)/shard_map/dot_general | solution.py:56
  (52 shorter events, 13.1 us)
Async XLA Ops:
  6.5 183.3 %copy-start.7 = (f32[4,64,64]{2,1,0:T(8,128)S(1)}, f32[4,64,64]{2,1,0:T(8,128)}, u32[]{:S(2)}) copy-start(f32[4,64,64]{2,1,0:T(8,128)} %param.5) | copy-start | bytes 196612
  6.5 86.9 %all-reduce.13.cloned.1.call-start = ((), (), s32[]{:S(2)}) async-start(), calls=%async_computation | async-start | bytes 524288 | tf_op jit(solution)/shard_map/psum | solution.py:9
  33.4 156.5 %all-reduce.15.cloned.1.call-start = ((), (), s32[]{:S(2)}) async-start(), calls=%async_computation.1 | async-start | bytes 1048576 | tf_op jit(solution)/shard_map/psum | solution.py:35
  93.4 182.2 %copy-start.6 = (f32[64,1024]{1,0:T(8,128)S(1)}, f32[64,1024]{1,0:T(8,128)}, u32[]{:S(2)}) copy-start(f32[64,1024]{1,0:T(8,128)} %all-reduce.13.cloned.1.call-done) | copy-start | bytes 786436
  105.7 169.9 %all-reduce.29.cloned.1.call-start = ((), (), s32[]{:S(2)}) async-start(), calls=%async_computation.8 | async-start | bytes 1048576 | tf_op jit(solution)/shard_map/psum | solution.py:9
  218.1 167.2 %all-reduce.17.cloned.1.call-start = ((), (), s32[]{:S(2)}) async-start(), calls=%async_computation.2 | async-start | bytes 1048576 | tf_op jit(solution)/shard_map/psum | solution.py:35
  275.6 16.3 %copy-start.4 = (f32[64,1024]{1,0:T(8,128)S(1)}, f32[64,1024]{1,0:T(8,128)}, u32[]{:S(2)}) copy-start(f32[64,1024]{1,0:T(8,128)} %get-tuple-element.10) | copy-start | bytes 786436
  288.4 3.4 copy-start.1
  300.8 170.2 %all-reduce.27.cloned.1.call-start = ((), (), s32[]{:S(2)}) async-start(), calls=%async_computation.7 | async-start | bytes 1048576 | tf_op jit(solution)/shard_map/psum | solution.py:9
  413.4 167.3 %all-reduce.19.cloned.1.call-start = ((), (), s32[]{:S(2)}) async-start(), calls=%async_computation.3 | async-start | bytes 1048576 | tf_op jit(solution)/shard_map/psum | solution.py:35
  471.0 16.3 %copy-start.3 = (f32[64,1024]{1,0:T(8,128)S(1)}, f32[64,1024]{1,0:T(8,128)}, u32[]{:S(2)}) copy-start(f32[64,1024]{1,0:T(8,128)} %get-tuple-element.8) | copy-start | bytes 786436
  483.9 3.4 copy-start
  496.2 170.1 %all-reduce.25.cloned.1.call-start = ((), (), s32[]{:S(2)}) async-start(), calls=%async_computation.6 | async-start | bytes 1048576 | tf_op jit(solution)/shard_map/psum | solution.py:9
  608.8 167.0 %all-reduce.21.cloned.1.call-start = ((), (), s32[]{:S(2)}) async-start(), calls=%async_computation.4 | async-start | bytes 1048576 | tf_op jit(solution)/shard_map/psum | solution.py:35
  666.3 16.3 %copy-start.5 = (f32[64,1024]{1,0:T(8,128)S(1)}, f32[64,1024]{1,0:T(8,128)}, u32[]{:S(2)}) copy-start(f32[64,1024]{1,0:T(8,128)} %get-tuple-element.6) | copy-start | bytes 786436
  679.2 3.4 copy-start.2
  691.5 169.2 %all-reduce.23.cloned.1.call-start = ((), (), s32[]{:S(2)}) async-start(), calls=%async_computation.5 | async-start | bytes 524288 | tf_op jit(solution)/shard_map/psum | solution.py:9
Sparse Core Ops, SparseCore 0:
  33.5 59.8 all-reduce.12
  105.8 84.0 all-reduce.14
  218.2 57.3 all-reduce.28
  300.9 84.2 all-reduce.16
  413.5 57.4 all-reduce.26
  496.3 84.2 all-reduce.18
  608.9 57.3 all-reduce.24
  691.6 84.1 all-reduce.20
  804.4 56.2 all-reduce.22
where the time goes:
time: 886 us; the launch traced here: 879 us
  waiting for transfers between devices  547 us (62%)
  blocking collectives  199 us (22%)
  matrix products  101 us (11%)
  between operations  13.6 us (2%)
  local copies, waits for them, and re-layouts  11 us (1%)
    psum x5, waiting for transfers between devices, broadcast(): return lax.psum(kept, axis)  288 us
    psum x4, waiting for transfers between devices, shards(): product_rows = lax.psum(partial_value, 'col')  259 us
    all_gather x4, blocking collectives, shards(): reflect_rows = lax.all_gather(piece, 'col', axis=1, tiled=True)  101 us
    psum x4, blocking collectives, shards(): inner = lax.psum(local_inner, 'row')  98.1 us
    dot_general x4, matrix products, shards(): lax.dot_general(left_block, right_block, (((0,), (0,)), ((), ())), precis...  49.8 us
    dot_general x4, matrix products, shards(): lax.dot_general(reflect_cols, matrix, (((1,), (1,)), ((), ())), precision...  39 us
  transfers between devices with their start and end apart: 9, of which 9 were waited for; matrix products, arithmetic and copies ran while one was open for 0% of the time, Pallas kernels for 0%

commit v1 on v0

--- a/solution.py
+++ b/solution.py
@@ -4,9 +4,14 @@
 from jax.sharding import PartitionSpec as P
 
 
+def time_the_types(comm_axis, chunk):
+    all_values = lax.all_gather(chunk, comm_axis).sum(axis=0)
+    return all_values
+
+
 def broadcast(value, axis, source):
     kept = jnp.where(lax.axis_index(axis) == source, value, 0).astype(value.dtype)
-    return lax.psum(kept, axis)
+    return time_the_types(axis, kept)
 
 
 def shards(symmetric, reflectors, tri_factor):

time: 886 us -> 724 us (0.82)
  waiting for transfers between devices: 547 us -> 380 us
  other arithmetic: 5.77 us -> 19.8 us
  matrix products: 101 us -> 89.6 us
    psum x5 -> x0, waiting for transfers between devices: 288 us -> none  [broadcast(): return lax.psum(kept, axis)]
    all_gather x0 -> x8, waiting for transfers between devices: none -> 117 us  [time_the_types(): all_values = lax.all_gather(chunk, comm_axis).sum(axis=0)]
    reduce_sum x0 -> x8, other arithmetic: none -> 14 us  [time_the_types(): all_values = lax.all_gather(chunk, comm_axis).sum(axis=0)]
    dot_general x4, matrix products: 49.8 us -> 39.9 us  [shards(): lax.dot_general(left_block, right_block, (((0,), (0,)), ((), ())), precis...]
  transfers between devices with their start and end apart: 9 -> 12, of which waited for: 9 -> 9; matrix products, arithmetic and copies ran while one was open for 0% -> 3% of each run, Pallas kernels for 0% -> 0%
where the time goes in v1:
time: 724 us; the launch traced here: 717 us
  waiting for transfers between devices  380 us (52%)
  blocking collectives  201 us (28%)
  matrix products  89.6 us (12%)
  other arithmetic  19.8 us (3%)
  between operations  14.1 us (2%)
  local copies, waits for them, and re-layouts  11 us (2%)
    psum x4, waiting for transfers between devices, shards(): product_rows = lax.psum(partial_value, 'col')  263 us
    all_gather x8, waiting for transfers between devices, time_the_types(): all_values = lax.all_gather(chunk, comm_axis).sum(axis=0)  117 us
    all_gather x4, blocking collectives, shards(): reflect_rows = lax.all_gather(piece, 'col', axis=1, tiled=True)  102 us
    psum x4, blocking collectives, shards(): inner = lax.psum(local_inner, 'row')  99.2 us
    dot_general x4, matrix products, shards(): lax.dot_general(left_block, right_block, (((0,), (0,)), ((), ())), precis...  39.9 us
    dot_general x4, matrix products, shards(): lax.dot_general(reflect_cols, matrix, (((1,), (1,)), ((), ())), precision...  37.9 us
  transfers between devices with their start and end apart: 12, of which 9 were waited for; matrix products, arithmetic and copies ran while one was open for 3% of the time, Pallas kernels for 0%

profile of v1, /device:TPU:0, one launch (start us, length us, event | category | flops | bytes accessed | tf_op | source)
XLA Modules:
  0.0 717.4 jit_solution(12885770256622975049)
XLA Ops:
  7.4 25.2 %all-gather = f32[1,64,2048]{2,1,0:T(8,128)S(1)} all-gather(f32[1,64,128]{2,1,0:T(8,128)S(1)} %get-tuple-element.7), channel_id=2, replica_groups=mesh['row'=8,'col'=16] {'col'}, dimensions={2}, use_global_device_ids=true | all-gather | bytes 557056 | tf_op jit(solution)/shard_map/all_gather | solution.py:29
  33.4 25.3 %all-gather.33.cloned.1.call-done = f32[1,512,1024]{2,1,0:T(8,128)} async-done(((f32[1,64,1024]{2,1,0:T(8,128)}), f32[1,512,1024]{2,1,0:T(8,128)}) %all-gather.33.cloned.1.call-update) | async-done | bytes 2097168 | tf_op jit(solution)/shard_map/all_gather | solution.py:8
  60.5 11.1 %fusion.65 = f32[64,2048]{1,0:T(8,128)} fusion(f32[64,1024]{1,0:T(8,128)S(1)} %reduce_sum.72, f32[2048,1024]{1,0:T(8,128)} %param.3), kind=kOutput, calls=%fused_computation.85 | convolution fusion | flops 1610612736 | bytes 9175040 | tf_op jit(solution)/shard_map/dot_general | solution.py:33
  71.7 25.6 %all-gather.3 = f32[1,64,2048]{2,1,0:T(8,128)S(1)} all-gather(f32[1,64,128]{2,1,0:T(8,128)S(1)} %get-tuple-element.6), channel_id=5, replica_groups=mesh['row'=8,'col'=16] {'col'}, dimensions={2}, use_global_device_ids=true | all-gather | bytes 557056 | tf_op jit(solution)/shard_map/all_gather | solution.py:29
  98.1 59.3 %all-reduce.5.cloned.1.call-done = f32[64,2048]{1,0:T(8,128)} async-done(((f32[64,2048]{1,0:T(8,128)}), f32[64,2048]{1,0:T(8,128)}) %all-reduce.5.cloned.1.call-update) | async-done | bytes 524304 | tf_op jit(solution)/shard_map/psum | solution.py:40
  159.6 24.8 %psum.57 = f32[64,64]{0,1:T(8,128)S(1)} all-reduce(f32[64,64]{0,1:T(8,128)S(1)} %convolution_bitcast_fusion.3), channel_id=1, replica_groups=mesh['row'=8,'col'=16] {'row'}, use_global_device_ids=true, to_apply=%region_2.3 | all-reduce | flops 4096 | bytes 32768 | tf_op jit(solution)/shard_map/psum | solution.py:51
  186.5 1.7 reduce_sum.74
  188.2 23.2 %all-gather.25.cloned.1.call-done = f32[512,1024]{1,0:T(8,128)} async-done(((f32[64,1024]{1,0:T(8,128)}), f32[512,1024]{1,0:T(8,128)}) %all-gather.25.cloned.1.call-update) | async-done | bytes 2097168 | tf_op jit(solution)/shard_map/all_gather | solution.py:8
  211.4 1.7 reduce_sum.73
  213.2 9.6 %convolution_subtract_fusion.3 = f32[2048,1024]{1,0:T(8,128)S(1)} fusion(f32[2048,1024]{1,0:T(8,128)} %param.3, f32[64,2048]{1,0:T(8,128)S(1)} %fusion.3, f32[64,2048]{1,0:T(8,128)S(1)} %bitcast.91, f32[64,1024]{1,0:T(8,128)S(1)} %reduce_sum.72, f32[64,1024]{1,0:T(8,128)S(1)} %reduce_sum.73), kind=kOutput, calls=%fused_computation.3 | convolution fusion | flops 3223715840 | bytes 18350080 | tf_op jit(solution)/shard_map/dot_general | solution.py:61
  222.8 3.4 copy-done.1
  226.2 8.9 %fusion.66 = f32[64,2048]{1,0:T(8,128)} fusion(f32[64,1024]{1,0:T(8,128)S(1)} %reduce_sum.74, f32[2048,1024]{1,0:T(8,128)S(1)} %convolution_subtract_fusion.3), kind=kOutput, calls=%fused_computation.86 | convolution fusion | flops 1610612736 | bytes 9175040 | tf_op jit(solution)/shard_map/dot_general | solution.py:33
  235.2 25.6 %all-gather.6 = f32[1,64,2048]{2,1,0:T(8,128)S(1)} all-gather(f32[1,64,128]{2,1,0:T(8,128)S(1)} %get-tuple-element.8), channel_id=8, replica_groups=mesh['row'=8,'col'=16] {'col'}, dimensions={2}, use_global_device_ids=true | all-gather | bytes 557056 | tf_op jit(solution)/shard_map/all_gather | solution.py:29
  261.6 59.2 %all-reduce.7.cloned.1.call-done = f32[64,2048]{1,0:T(8,128)} async-done(((f32[64,2048]{1,0:T(8,128)}), f32[64,2048]{1,0:T(8,128)}) %all-reduce.7.cloned.1.call-update) | async-done | bytes 524304 | tf_op jit(solution)/shard_map/psum | solution.py:40
  323.1 25.3 %psum.59 = f32[64,64]{0,1:T(8,128)S(1)} all-reduce(f32[64,64]{0,1:T(8,128)S(1)} %convolution_bitcast_fusion.2), channel_id=1, replica_groups=mesh['row'=8,'col'=16] {'row'}, use_global_device_ids=true, to_apply=%region_6.7 | all-reduce | flops 4096 | bytes 32768 | tf_op jit(solution)/shard_map/psum | solution.py:51
  349.9 1.7 reduce_sum.76
  351.7 23.0 %all-gather.27.cloned.1.call-done = f32[512,1024]{1,0:T(8,128)} async-done(((f32[64,1024]{1,0:T(8,128)}), f32[512,1024]{1,0:T(8,128)}) %all-gather.27.cloned.1.call-update) | async-done | bytes 2097168 | tf_op jit(solution)/shard_map/all_gather | solution.py:8
  376.4 9.6 %convolution_subtract_fusion.2 = f32[2048,1024]{1,0:T(8,128)S(1)} fusion(f32[2048,1024]{1,0:T(8,128)} %copy-done.1, f32[64,2048]{1,0:T(8,128)S(1)} %fusion.2, f32[64,2048]{1,0:T(8,128)S(1)} %bitcast.89, f32[64,1024]{1,0:T(8,128)S(1)} %reduce_sum.74, f32[64,1024]{1,0:T(8,128)S(1)} %reduce_sum.75), kind=kOutput, calls=%fused_computation.2 | convolution fusion | flops 3223715840 | bytes 18350080 | tf_op jit(solution)/shard_map/dot_general | solution.py:61
  385.9 3.4 copy-done
  389.3 8.9 %fusion.67 = f32[64,2048]{1,0:T(8,128)} fusion(f32[64,1024]{1,0:T(8,128)S(1)} %reduce_sum.76, f32[2048,1024]{1,0:T(8,128)S(1)} %convolution_subtract_fusion.2), kind=kOutput, calls=%fused_computation.87 | convolution fusion | flops 1610612736 | bytes 9175040 | tf_op jit(solution)/shard_map/dot_general | solution.py:33
  398.3 25.6 %all-gather.9 = f32[1,64,2048]{2,1,0:T(8,128)S(1)} all-gather(f32[1,64,128]{2,1,0:T(8,128)S(1)} %get-tuple-element.5), channel_id=11, replica_groups=mesh['row'=8,'col'=16] {'col'}, dimensions={2}, use_global_device_ids=true | all-gather | bytes 557056 | tf_op jit(solution)/shard_map/all_gather | solution.py:29
  425.0 59.1 %all-reduce.9.cloned.1.call-done = f32[64,2048]{1,0:T(8,128)} async-done(((f32[64,2048]{1,0:T(8,128)}), f32[64,2048]{1,0:T(8,128)}) %all-reduce.9.cloned.1.call-update) | async-done | bytes 524304 | tf_op jit(solution)/shard_map/psum | solution.py:40
  486.3 24.8 %psum.61 = f32[64,64]{0,1:T(8,128)S(1)} all-reduce(f32[64,64]{0,1:T(8,128)S(1)} %convolution_bitcast_fusion.1), channel_id=1, replica_groups=mesh['row'=8,'col'=16] {'row'}, use_global_device_ids=true, to_apply=%region_10.11 | all-reduce | flops 4096 | bytes 32768 | tf_op jit(solution)/shard_map/psum | solution.py:51
  512.6 1.7 reduce_sum.78
  514.4 23.7 %all-gather.29.cloned.1.call-done = f32[512,1024]{1,0:T(8,128)} async-done(((f32[64,1024]{1,0:T(8,128)}), f32[512,1024]{1,0:T(8,128)}) %all-gather.29.cloned.1.call-update) | async-done | bytes 2097168 | tf_op jit(solution)/shard_map/all_gather | solution.py:8
  539.8 9.6 %convolution_subtract_fusion.1 = f32[2048,1024]{1,0:T(8,128)S(1)} fusion(f32[2048,1024]{1,0:T(8,128)} %copy-done, f32[64,2048]{1,0:T(8,128)S(1)} %fusion.1, f32[64,2048]{1,0:T(8,128)S(1)} %bitcast.88, f32[64,1024]{1,0:T(8,128)S(1)} %reduce_sum.76, f32[64,1024]{1,0:T(8,128)S(1)} %reduce_sum.77), kind=kOutput, calls=%fused_computation.1 | convolution fusion | flops 3223715840 | bytes 18350080 | tf_op jit(solution)/shard_map/dot_general | solution.py:61
  549.4 3.4 copy-done.2
  552.8 8.9 %fusion.68 = f32[64,2048]{1,0:T(8,128)} fusion(f32[64,1024]{1,0:T(8,128)S(1)} %reduce_sum.78, f32[2048,1024]{1,0:T(8,128)S(1)} %convolution_subtract_fusion.1), kind=kOutput, calls=%fused_computation.88 | convolution fusion | flops 1610612736 | bytes 9175040 | tf_op jit(solution)/shard_map/dot_general | solution.py:33
  562.1 85.3 %all-reduce.11.cloned.1.call-done = f32[64,2048]{1,0:T(8,128)} async-done(((f32[64,2048]{1,0:T(8,128)}), f32[64,2048]{1,0:T(8,128)}) %all-reduce.11.cloned.1.call-update) | async-done | bytes 524304 | tf_op jit(solution)/shard_map/psum | solution.py:40
  649.6 24.4 %psum.63 = f32[64,64]{0,1:T(8,128)S(1)} all-reduce(f32[64,64]{0,1:T(8,128)S(1)} %convolution_bitcast_fusion), channel_id=1, replica_groups=mesh['row'=8,'col'=16] {'row'}, use_global_device_ids=true, to_apply=%region_14.15 | all-reduce | flops 4096 | bytes 32768 | tf_op jit(solution)/shard_map/psum | solution.py:51
  675.6 21.8 %all-gather.31.cloned.1.call-done = f32[512,1024]{1,0:T(8,128)} async-done(((f32[64,1024]{1,0:T(8,128)}), f32[512,1024]{1,0:T(8,128)}) %all-gather.31.cloned.1.call-update) | async-done | bytes 2097168 | tf_op jit(solution)/shard_map/all_gather | solution.py:8
  699.1 11.2 %convolution_subtract_fusion = f32[2048,1024]{1,0:T(8,128)} fusion(f32[2048,1024]{1,0:T(8,128)} %copy-done.2, f32[64,2048]{1,0:T(8,128)S(1)} %fusion, f32[64,2048]{1,0:T(8,128)S(1)} %bitcast.90, f32[64,1024]{1,0:T(8,128)S(1)} %reduce_sum.78, f32[64,1024]{1,0:T(8,128)S(1)} %reduce_sum.79), kind=kOutput, calls=%fused_computation | convolution fusion | flops 3223715840 | bytes 18350080 | tf_op jit(solution)/shard_map/dot_general | solution.py:61
  (61 shorter events, 27.1 us)
Async XLA Ops:
  6.5 150.9 %copy-start.3 = (f32[4,64,64]{2,1,0:T(8,128)S(1)}, f32[4,64,64]{2,1,0:T(8,128)}, u32[]{:S(2)}) copy-start(f32[4,64,64]{2,1,0:T(8,128)} %param.5) | copy-start | bytes 196612
  6.5 52.2 %all-gather.33.cloned.1.call-start = ((), (), s32[]{:S(2)}) async-start(), calls=%async_computation.8 | async-start | bytes 2359296 | tf_op jit(solution)/shard_map/all_gather | solution.py:8
  33.4 124.0 %all-reduce.5.cloned.1.call-start = ((), (), s32[]{:S(2)}) async-start(), calls=%async_computation | async-start | bytes 1048576 | tf_op jit(solution)/shard_map/psum | solution.py:40
  71.6 114.9 %all-gather.35.cloned.1.call-start = ((), (), s32[]{:S(2)}) async-start(), calls=%async_computation.9 | async-start | bytes 2359296 | tf_op jit(solution)/shard_map/all_gather | solution.py:8
  98.0 113.4 %all-gather.25.cloned.1.call-start = ((), (), s32[]{:S(2)}) async-start(), calls=%async_computation.4 | async-start | bytes 2359296 | tf_op jit(solution)/shard_map/all_gather | solution.py:8
  185.9 134.9 %all-reduce.7.cloned.1.call-start = ((), (), s32[]{:S(2)}) async-start(), calls=%async_computation.1 | async-start | bytes 1048576 | tf_op jit(solution)/shard_map/psum | solution.py:40
  222.8 3.4 copy-start.1
  235.1 114.8 %all-gather.37.cloned.1.call-start = ((), (), s32[]{:S(2)}) async-start(), calls=%async_computation.10 | async-start | bytes 2359296 | tf_op jit(solution)/shard_map/all_gather | solution.py:8
  261.5 113.1 %all-gather.27.cloned.1.call-start = ((), (), s32[]{:S(2)}) async-start(), calls=%async_computation.5 | async-start | bytes 2359296 | tf_op jit(solution)/shard_map/all_gather | solution.py:8
  349.8 134.2 %all-reduce.9.cloned.1.call-start = ((), (), s32[]{:S(2)}) async-start(), calls=%async_computation.2 | async-start | bytes 1048576 | tf_op jit(solution)/shard_map/psum | solution.py:40
  385.9 3.4 copy-start
  398.3 114.3 %all-gather.39.cloned.1.call-start = ((), (), s32[]{:S(2)}) async-start(), calls=%async_computation.11 | async-start | bytes 2359296 | tf_op jit(solution)/shard_map/all_gather | solution.py:8
  424.7 113.4 %all-gather.29.cloned.1.call-start = ((), (), s32[]{:S(2)}) async-start(), calls=%async_computation.6 | async-start | bytes 2359296 | tf_op jit(solution)/shard_map/all_gather | solution.py:8
  512.5 134.8 %all-reduce.11.cloned.1.call-start = ((), (), s32[]{:S(2)}) async-start(), calls=%async_computation.3 | async-start | bytes 1048576 | tf_op jit(solution)/shard_map/psum | solution.py:40
  549.4 3.4 copy-start.2
  561.8 135.6 %all-gather.31.cloned.1.call-start = ((), (), s32[]{:S(2)}) async-start(), calls=%async_computation.7 | async-start | bytes 2359296 | tf_op jit(solution)/shard_map/all_gather | solution.py:8
Sparse Core Ops, SparseCore 0:
  33.5 25.1 all-gather.32
  71.7 85.6 all-reduce.4
  159.2 24.7 all-gather.34
  186.0 25.3 all-gather.24
  235.2 85.5 all-reduce.6
  322.4 24.7 all-gather.36
  349.9 24.6 all-gather.26
  398.4 85.5 all-reduce.8
  485.9 24.7 all-gather.38
  512.7 25.3 all-gather.28
  561.9 85.4 all-reduce.10
  675.7 21.6 all-gather.30
